TPU v7x, 32 devices: a whole 2x2x4 slice. The times are simulated.
32 devices in a mesh: tm: 4 (over x, core), space: 8 (over z, y).
Axes of the slice: x: 2, y: 2, z: 4, core: 2. Of those that a mesh axis runs over, the one named last changes fastest.
Arguments:
- video_in: bfloat16 [16, 8, 16, 3072], P('tm', 'space'), may hold values from -6 to 6
- neighbours: int32 [8, 8], replicated, may hold values from 0 to 8, as said below
- valid_frames: int32 [8], replicated, may hold values from 0 to 16, as said below
- norm1_gain: float32 [192], replicated, may hold values from 0.1 to 1.9
- conv1_weight: bfloat16 [9, 576, 192], replicated, may hold values from -0.078125 to 0.078125
- conv1_bias: float32 [192], replicated, may hold values from -3 to 3
- norm2_gain: float32 [192], replicated, may hold values from 0.1 to 1.9
- conv2_weight: bfloat16 [9, 576, 192], replicated, may hold values from -0.078125 to 0.078125
- conv2_bias: float32 [192], replicated, may hold values from -3 to 3
Outputs:
- block_out: bfloat16 [16, 8, 16, 3072], P('tm', 'space')
Inputs may be any that keep to these rules, and one draw needn't show every extreme that they name: `neighbours`: entry k of a tile's row names the tile beside it in direction k of one placement of all tiles on a grid of 1 row by 8 columns, directions ordered (row, column) = (-1,-1), (-1,0), (-1,1), (0,-1), (0,1), (1,-1), (1,0), (1,1); 8 where that place lies outside the grid. `valid_frames`: frames from this number on are padding in that tile's track.
All inputs are finite; a program needn't handle non-finite values.
Results may differ from a plain program's by a relative error of at most 0.0037.
Values may be sent and summed in bfloat16 or wider, within the bound.
No kernel may reach another device: no remote copies, remote signals or barrier semaphores. Data moves between devices by JAX's collectives and lax.ppermute only.
A program may use at most 64 MiB of HBM per device.

v0:
```python
from functools import partial
import jax
import jax.numpy as jnp
from jax import lax
from jax.sharding import PartitionSpec as P

epsilon = 1e-06


def shifted(value, axis, steps):
    count = lax.axis_size(axis)
    first, last = (max(0, -steps), min(count, count - steps))
    return lax.ppermute(value, axis, [(source, source + steps) for source in range(first, last)])


def norm_silu(values, scale_gain):
    square = jnp.mean(values * values, axis=-1, keepdims=True)
    return jax.nn.silu(values * lax.rsqrt(square + epsilon) * scale_gain)


def conv_tile(framed, weight):
    frames_out = framed.shape[0] - 2
    side_len = framed.shape[1] - 2
    channels = framed.shape[-1]
    widened = jnp.concatenate(
        [framed[:, :, col_off : col_off + side_len] for col_off in range(3)], axis=-1
    )
    summed = jnp.zeros((frames_out * side_len * side_len, channels), jnp.float32)
    for time_off in range(3):
        for row_off in range(3):
            window = widened[
                time_off : time_off + frames_out, row_off : row_off + side_len
            ].reshape(-1, 3 * channels)
            summed = summed + jnp.dot(
                window, weight[time_off * 3 + row_off], preferred_element_type=jnp.float32
            )
    return summed.reshape(frames_out, side_len, side_len, channels)


def edge_pack(activation):
    return jnp.stack(
        [
            activation[:, :, -1],
            activation[:, :, :, -1],
            activation[:, :, :, 0],
            activation[:, :, 0],
        ],
        axis=2,
    )


def fold_edges(totals, portion, offset, nearby):
    amount = portion.shape[1]
    tile_ids = jnp.arange(amount, dtype=jnp.int32)
    choose = (nearby[:, :, None] == tile_ids[None, None, :]).astype(jnp.bfloat16)
    side_choose = jnp.stack([choose[:, 1], choose[:, 3], choose[:, 4], choose[:, 6]], axis=1)
    corner_choose = jnp.stack([choose[:, 0], choose[:, 2], choose[:, 5], choose[:, 7]], axis=1)
    corner_source = jnp.stack(
        [portion[:, :, 0, -1], portion[:, :, 0, 0], portion[:, :, 3, -1], portion[:, :, 3, 0]],
        axis=2,
    )
    new_sides = jnp.einsum(
        "djn,fnjxc->fdjxc", side_choose, portion, preferred_element_type=jnp.float32
    )
    new_corners = jnp.einsum(
        "djn,fnjc->fdjc", corner_choose, corner_source, preferred_element_type=jnp.float32
    )
    return (new_sides.astype(jnp.bfloat16), new_corners.astype(jnp.bfloat16))


def empty_rims(frame_count, activation):
    tiles_dev, side_len, channels = (activation.shape[1], activation.shape[2], activation.shape[4])
    return (
        jnp.zeros((frame_count, tiles_dev, 4, side_len, channels), jnp.bfloat16),
        jnp.zeros((frame_count, tiles_dev, 4, channels), jnp.bfloat16),
    )


def assemble(longer, side_rims, corners):
    top_row = jnp.concatenate([corners[:, :, 0:1], side_rims[:, :, 0], corners[:, :, 1:2]], axis=2)
    bottom_row = jnp.concatenate(
        [corners[:, :, 2:3], side_rims[:, :, 3], corners[:, :, 3:4]], axis=2
    )
    middle = jnp.concatenate(
        [side_rims[:, :, 1][:, :, :, None], longer, side_rims[:, :, 2][:, :, :, None]], axis=3
    )
    return jnp.concatenate([top_row[:, :, None], middle, bottom_row[:, :, None]], axis=2)


def extend(activation, nearby):
    frames_dev = activation.shape[0]
    folder = partial(fold_edges, nearby=nearby)
    side_rims, corners = folder(
        empty_rims(frames_dev, activation),
        lax.all_gather(edge_pack(activation), "space", axis=1, tiled=True),
        jnp.int32(0),
    )
    prev_act, prev_sides, prev_corners = shifted(
        (activation[frames_dev - 2 :], side_rims[frames_dev - 2 :], corners[frames_dev - 2 :]),
        "tm",
        1,
    )
    longer = jnp.concatenate([prev_act, activation], axis=0)
    side_rims = jnp.concatenate([prev_sides, side_rims], axis=0)
    corners = jnp.concatenate([prev_corners, corners], axis=0)
    return assemble(longer, side_rims, corners)


def blank_tile(pieces, tile_valid):
    framed = pieces[0]
    return jnp.zeros(
        (framed.shape[0] - 2, framed.shape[1] - 2, framed.shape[2] - 2, framed.shape[3]),
        jnp.bfloat16,
    )


def home_tiles(inputs, home_valid, first_frame, worker):
    pieces = tuple((stacked[:, 0] for stacked in inputs))
    results = [lax.cond(home_valid[0] > first_frame, worker, blank_tile, pieces, home_valid[0])]
    return jnp.stack(results, axis=1)


def on_device(
    video_in,
    neighbours,
    valid_frames,
    norm1_gain,
    conv1_weight,
    conv1_bias,
    norm2_gain,
    conv2_weight,
    conv2_bias,
):
    frames_dev, tiles_dev, side_len, merged = video_in.shape
    channels = norm1_gain.shape[0]
    voxels = video_in.reshape(frames_dev, tiles_dev, side_len, side_len, channels)
    first_frame = lax.axis_index("tm") * frames_dev
    home_ids = lax.axis_index("space") * tiles_dev + jnp.arange(tiles_dev, dtype=jnp.int32)
    home_valid = jnp.take(valid_frames, home_ids)
    nearby = jnp.take(neighbours, home_ids, axis=0)
    frame_pos = first_frame + jnp.arange(frames_dev, dtype=jnp.int32)
    present = (frame_pos[:, None] < home_valid[None, :]).astype(jnp.bfloat16)
    masked = voxels * present[:, :, None, None, None]
    activation = norm_silu(masked.astype(jnp.float32), norm1_gain).astype(jnp.bfloat16)

    def frame_weights(tile_valid):
        return (frame_pos < tile_valid).astype(jnp.float32)[:, None, None, None]

    def first_worker(pieces, tile_valid):
        summed = conv_tile(pieces[0], conv1_weight)
        return norm_silu((summed + conv1_bias) * frame_weights(tile_valid), norm2_gain).astype(
            jnp.bfloat16
        )

    def second_worker(pieces, tile_valid):
        summed = conv_tile(pieces[0], conv2_weight)
        return (
            (summed + conv2_bias) * frame_weights(tile_valid) + pieces[1].astype(jnp.float32)
        ).astype(jnp.bfloat16)

    padded = extend(activation, nearby)
    hidden = home_tiles((padded,), home_valid, first_frame, first_worker)
    padded = extend(hidden, nearby)
    block_out = home_tiles((padded, masked), home_valid, first_frame, second_worker)
    return block_out.reshape(frames_dev, tiles_dev, side_len, side_len * channels)


def solution(mesh):
    in_specs = (P("tm", "space", None, None), P(), P(), P(), P(), P(), P(), P(), P())
    out_specs = P("tm", "space", None, None)
    return jax.shard_map(
        on_device, mesh=mesh, in_specs=in_specs, out_specs=out_specs, check_vma=False
    )
```

profile of v0, /device:TPU:1, one launch (start us, length us, event | category | flops | bytes accessed | tf_op | source)
XLA Modules:
  0.0 148.6 jit_solution(2349354967583737358)
XLA Ops:
  0.0 1.6 %reshape.252 = bf16[4,1,16,16,192]{4,3,2,0,1:T(8,128)(2,1)S(1)} reshape(bf16[4,1,16,3072]{3,2,1,0:T(8,128)(2,1)} %param.13) | data formatting | bytes 786432 | tf_op jit(solution)/shard_map/reshape | solution.py:136
  1.6 1.2 dynamic-slice.5
  3.7 0.4 fusion.9
  4.4 28.5 %all_gather.6 = bf16[4,8,4,16,192]{4,3,2,0,1:T(8,128)(2,1)S(1)} all-gather(bf16[4,1,4,16,192]{4,3,2,0,1:T(8,128)(2,1)S(1)} %pad_maximum_fusion.4), channel_id=1, replica_groups=mesh['tm'=4,'space'=8] {'space'}, dimensions={1}, use_global_device_ids=true | all-gather | bytes 884736 | tf_op jit(solution)/shard_map/all_gather | solution.py:95
  33.0 0.7 fusion.69
  34.0 9.1 %collective-permute-start = (bf16[2,1,4,192]{3,2,0,1:T(4,128)(2,1)S(1)}, bf16[2,1,4,192]{3,2,0,1:T(4,128)(2,1)S(1)}, u32[]{:S(2)}, u32[]{:S(2)}) collective-permute-start(bf16[2,1,4,192]{3,2,0,1:T(4,128)(2,1)S(1)} %slice.382), channel_id=1, source_target_pairs={{0,8},{8,16},{16,24},{1,9},{9,17},{17,25},{2,10},{10,18},{18,26},{... | collective-permute-start | bytes 9224 | tf_op jit(solution)/shard_map/ppermute | solution.py:13
  43.2 0.7 fusion.12
  43.9 1.9 %collective-permute-start.1 = (bf16[2,1,4,16,192]{4,3,0,2,1:T(8,128)(2,1)S(1)}, bf16[2,1,4,16,192]{4,3,0,2,1:T(8,128)(2,1)S(1)}, u32[]{:S(2)}, u32[]{:S(2)}) collective-permute-start(bf16[2,1,4,16,192]{4,3,0,2,1:T(8,128)(2,1)S(1)} %slice.385), channel_id=1, source_target_pairs={{0,8},{8,16},{16,24},{1,9},{9,17},{17,25},{2,10},{10,18},{18,26},{... | collective-permute-start | bytes 147464 | tf_op jit(solution)/shard_map/ppermute | solution.py:13
  45.9 1.9 %collective-permute-start.2 = (bf16[2,1,16,16,192]{4,3,2,0,1:T(8,128)(2,1)S(1)}, bf16[2,1,16,16,192]{4,3,2,0,1:T(8,128)(2,1)S(1)}, u32[]{:S(2)}, u32[]{:S(2)}) collective-permute-start(bf16[2,1,16,16,192]{4,3,2,0,1:T(8,128)(2,1)S(1)} %slice.392), channel_id=1, source_target_pairs={{0,8},{8,16},{16,24},{1,9},{9,17},{17,25},{2,10},{10,18},{18,26},{... | collective-permute-start | bytes 589832 | tf_op jit(solution)/shard_map/ppermute | solution.py:13
  48.2 2.9 %collective-permute-done.2 = bf16[2,1,16,16,192]{4,3,2,0,1:T(8,128)(2,1)S(1)} collective-permute-done((bf16[2,1,16,16,192]{4,3,2,0,1:T(8,128)(2,1)S(1)}, bf16[2,1,16,16,192]{4,3,2,0,1:T(8,128)(2,1)S(1)}, u32[]{:S(2)}, u32[]{:S(2)}) %collective-permute-start.2) | collective-permute-done | bytes 196640 | tf_op jit(solution)/shard_map/ppermute | solution.py:13
  51.1 0.9 pad_maximum_fusion.2
  52.0 24.7 %conditional.2 = (bf16[4,16,16,192]{3,2,1,0:T(8,128)(2,1)S(1)}) conditional(s32[]{:T(128)} %convert_element_type.107, () %tuple.20, (bf16[6,1,18,18,192]{4,3,2,0,1:T(8,128)(2,1)S(1)}, bf16[9,576,192]{1,2,0:T(8,128)(2,1)}, f32[192]{0:T(256)S(1)}, s32[]{:T(128)}, s32[4]{0:T(128)S(1)}, /*index=5*/f32[192]{0:T(256)S(1)}) %tuple.102), branch_computations={%region_1.2_spmd, %region_2.4_spmd} | conditional | flops 2048533504 | bytes 96561936 | solution.py:119
  52.0 0.7 fusion.73
  52.7 0.9 pad_maximum_fusion
  53.6 4.4 %fusion.72 = (bf16[4,16,16,576]{3,2,1,0:T(8,128)(2,1)}, bf16[4,16,16,576]{3,2,1,0:T(8,128)(2,1)}, bf16[4,16,16,576]{3,2,1,0:T(8,128)(2,1)}, bf16[4,16,16,576]{3,...) fusion(bf16[6,18,16,576]{3,2,1,0:T(8,128)(2,1)S(1)} %pad_maximu, ...), kind=kLoop, calls=%fused_computation.174 | loop fusion | bytes 21233664 | tf_op jit(solution)/shard_map/cond/branch_1_fun/slice | solution.py:31
  58.0 4.1 %copy.179 = bf16[9,576,192]{2,1,0:T(8,128)(2,1)S(1)} copy(bf16[9,576,192]{1,2,0:T(8,128)(2,1)} %get-tuple-element.168) | data formatting | bytes 3981312 | tf_op jit(solution)/shard_map
  62.1 2.0 %fusion = f32[1024,192]{0,1:T(8,128)S(1)} fusion(bf16[1024,576]{1,0:T(8,128)(2,1)} %bitcast.249, bf16[9,576,192]{2,1,0:T(8,128)(2,1)S(1)} %copy.179), kind=kOutput, calls=%fused_computation.20 | convolution fusion | flops 226492416 | bytes 2260992 | tf_op jit(solution)/shard_map/cond/branch_1_fun/dot_general | solution.py:34
  64.2 0.6 convolution_add_fusion.7
  64.8 0.7 copy-done.11
  65.5 0.6 convolution_add_fusion.6
  66.1 0.7 copy-done.9
  66.8 0.6 convolution_add_fusion.5
  67.4 0.7 copy-done.7
  68.1 0.6 convolution_add_fusion.4
  68.7 0.7 copy-done.5
  69.4 0.6 convolution_add_fusion.3
  70.1 0.7 copy-done.3
  70.7 0.6 convolution_add_fusion.2
  71.4 0.7 copy-done.1
  72.1 1.5 %convolution_add_fusion.1 = f32[1024,192]{0,1:T(8,128)} fusion(f32[1024,192]{0,1:T(8,128)S(1)} %convolution_add_fusion.2, bf16[1024,576]{1,0:T(8,128)(2,1)S(1)} %bitcast.235, bf16[9,576,192]{2,1,0:T(8,128)(2,1)S(1)} %copy.179), kind=kOutput, calls=%fused_computation.2 | convolution fusion | flops 226689024 | bytes 3178496 | tf_op jit(solution)/shard_map/cond/branch_1_fun/dot_general | solution.py:34
  73.7 2.2 %multiply_reduce_fusion = (f32[1024]{0:T(1024)S(1)}, f32[1024,192]{0,1:T(8,128)S(1)}) fusion(f32[1024]{0:T(1024)S(1)} %mul.124, f32[192]{0:T(256)S(1)} %get-tuple-element.60, f32[1024,192]{0,1:T(8,128)} %convolution_add_fusion.1, bf16[1024,576]{1,0:T(8,128)(2,1)} %bitcast.233, bf16[9,576,192]{2,1,0:T(8,128)(2,1)S(1)} %copy.179), kind=kOutput, calls=%fused_computation.10 | convolution fusion | flops 227474432 | bytes 3056640 | tf_op jit(solution)/shard_map/cond/branch_1_fun/dot_general | solution.py:34
  75.9 0.3 copy.167
  76.3 0.4 multiply_convert_fusion
  77.0 29.7 %all_gather.7 = bf16[4,8,4,16,192]{4,3,2,0,1:T(8,128)(2,1)S(1)} all-gather(bf16[4,1,4,16,192]{4,3,2,0,1:T(8,128)(2,1)S(1)} %pad_maximum_fusion.5), channel_id=1, replica_groups=mesh['tm'=4,'space'=8] {'space'}, dimensions={1}, use_global_device_ids=true | all-gather | bytes 884736 | tf_op jit(solution)/shard_map/all_gather | solution.py:95
  106.8 0.7 fusion.10
  107.8 8.5 %collective-permute-start.3 = (bf16[2,1,4,192]{3,2,0,1:T(4,128)(2,1)S(1)}, bf16[2,1,4,192]{3,2,0,1:T(4,128)(2,1)S(1)}, u32[]{:S(2)}, u32[]{:S(2)}) collective-permute-start(bf16[2,1,4,192]{3,2,0,1:T(4,128)(2,1)S(1)} %slice.405), channel_id=1, source_target_pairs={{0,8},{8,16},{16,24},{1,9},{9,17},{17,25},{2,10},{10,18},{18,26},{... | collective-permute-start | bytes 9224 | tf_op jit(solution)/shard_map/ppermute | solution.py:13
  116.3 1.9 %collective-permute-start.4 = (bf16[2,1,4,16,192]{4,3,0,2,1:T(8,128)(2,1)S(1)}, bf16[2,1,4,16,192]{4,3,0,2,1:T(8,128)(2,1)S(1)}, u32[]{:S(2)}, u32[]{:S(2)}) collective-permute-start(bf16[2,1,4,16,192]{4,3,0,2,1:T(8,128)(2,1)S(1)} %slice.408), channel_id=1, source_target_pairs={{0,8},{8,16},{16,24},{1,9},{9,17},{17,25},{2,10},{10,18},{18,26},{... | collective-permute-start | bytes 147464 | tf_op jit(solution)/shard_map/ppermute | solution.py:13
  118.2 1.9 %collective-permute-start.5 = (bf16[2,1,16,16,192]{4,3,2,0,1:T(8,128)(2,1)S(1)}, bf16[2,1,16,16,192]{4,3,2,0,1:T(8,128)(2,1)S(1)}, u32[]{:S(2)}, u32[]{:S(2)}) collective-permute-start(bf16[2,1,16,16,192]{4,3,2,0,1:T(8,128)(2,1)S(1)} %slice_bitcast_fusion.36), channel_id=1, source_target_pairs={{0,8},{8,16},{16,24},{1,9},{9,17},{17,25},{2,10},{10,18},{18,26},{... | collective-permute-start | bytes 589832 | tf_op jit(solution)/shard_map/ppermute | solution.py:13
  120.5 2.9 %collective-permute-done.5 = bf16[2,1,16,16,192]{4,3,2,0,1:T(8,128)(2,1)S(1)} collective-permute-done((bf16[2,1,16,16,192]{4,3,2,0,1:T(8,128)(2,1)S(1)}, bf16[2,1,16,16,192]{4,3,2,0,1:T(8,128)(2,1)S(1)}, u32[]{:S(2)}, u32[]{:S(2)}) %collective-permute-start.5) | collective-permute-done | bytes 196640 | tf_op jit(solution)/shard_map/ppermute | solution.py:13
  123.5 0.9 pad_maximum_fusion.3
  124.3 24.3 %conditional.3 = (bf16[4,1,16,3072]{3,2,0,1:T(8,128)(2,1)}) conditional(s32[]{:T(128)} %convert_element_type.107, () %tuple.19, (bf16[6,1,18,18,192]{4,3,2,0,1:T(8,128)(2,1)S(1)}, bf16[9,576,192]{1,2,0:T(8,128)(2,1)}, f32[192]{0:T(256)S(1)}, s32[]{:T(128)}, s32[4]{0:T(128)S(1)}, /*index=5*/bf16[4]{0:T(256)(128)(2,1)S(1)}, ...), branch_computations={%region_4.5_spmd, %region_5.6_spmd} | conditional | flops 2047156224 | bytes 104957008 | solution.py:119
  124.4 0.7 fusion.75
  125.1 0.9 pad_maximum_fusion.1
  125.9 4.4 %fusion.74 = (bf16[4,16,16,576]{3,2,1,0:T(8,128)(2,1)}, bf16[4,16,16,576]{3,2,1,0:T(8,128)(2,1)}, bf16[4,16,16,576]{3,2,1,0:T(8,128)(2,1)}, bf16[4,16,16,576]{3,...) fusion(bf16[6,18,16,576]{3,2,1,0:T(8,128)(2,1)S(1)} %pad_maximu, ...), kind=kLoop, calls=%fused_computation.176 | loop fusion | bytes 21233664 | tf_op jit(solution)/shard_map/cond/branch_1_fun/slice | solution.py:31
  130.3 4.1 %copy.190 = bf16[9,576,192]{2,1,0:T(8,128)(2,1)S(1)} copy(bf16[9,576,192]{1,2,0:T(8,128)(2,1)} %get-tuple-element.174) | data formatting | bytes 3981312 | tf_op jit(solution)/shard_map
  134.4 2.0 %fusion.1 = f32[1024,192]{0,1:T(8,128)S(1)} fusion(bf16[1024,576]{1,0:T(8,128)(2,1)} %bitcast.250, bf16[9,576,192]{2,1,0:T(8,128)(2,1)S(1)} %copy.190), kind=kOutput, calls=%fused_computation.43 | convolution fusion | flops 226492416 | bytes 2260992 | tf_op jit(solution)/shard_map/cond/branch_1_fun/dot_general | solution.py:34
  136.5 0.6 convolution_add_fusion.15
  137.1 0.7 copy-done.12
  137.8 0.6 convolution_add_fusion.14
  138.4 0.7 copy-done.10
  139.1 0.6 convolution_add_fusion.13
  139.7 0.7 copy-done.8
  140.4 0.6 convolution_add_fusion.12
  141.1 0.7 copy-done.6
  141.8 0.6 convolution_add_fusion.11
  142.4 0.7 copy-done.4
  143.1 0.6 convolution_add_fusion.10
  143.7 0.7 copy-done.2
  144.4 0.6 convolution_add_fusion.9
  145.0 0.7 copy-done
  145.7 0.6 convolution_add_fusion.8
  146.7 0.4 reshape.248
  147.2 0.5 copy-done.15
  147.7 0.9 add_convert_fusion
  (91 shorter events, 2.8 us)
Async XLA Ops:
  0.0 3.7 %copy-start.17 = (f32[192]{0:T(256)S(1)}, f32[192]{0:T(256)}, u32[]{:S(2)}) copy-start(f32[192]{0:T(256)} %param.16) | copy-start | bytes 2308
  34.0 13.8 %collective-permute-start = (bf16[2,1,4,192]{3,2,0,1:T(4,128)(2,1)S(1)}, bf16[2,1,4,192]{3,2,0,1:T(4,128)(2,1)S(1)}, u32[]{:S(2)}, u32[]{:S(2)}) collective-permute-start(bf16[2,1,4,192]{3,2,0,1:T(4,128)(2,1)S(1)} %slice.382), channel_id=1, source_target_pairs={{0,8},{8,16},{16,24},{1,9},{9,17},{17,25},{2,10},{10,18},{18,26},{... | collective-permute-start | bytes 9224 | tf_op jit(solution)/shard_map/ppermute | solution.py:13
  43.9 4.0 %collective-permute-start.1 = (bf16[2,1,4,16,192]{4,3,0,2,1:T(8,128)(2,1)S(1)}, bf16[2,1,4,16,192]{4,3,0,2,1:T(8,128)(2,1)S(1)}, u32[]{:S(2)}, u32[]{:S(2)}) collective-permute-start(bf16[2,1,4,16,192]{4,3,0,2,1:T(8,128)(2,1)S(1)} %slice.385), channel_id=1, source_target_pairs={{0,8},{8,16},{16,24},{1,9},{9,17},{17,25},{2,10},{10,18},{18,26},{... | collective-permute-start | bytes 147464 | tf_op jit(solution)/shard_map/ppermute | solution.py:13
  45.9 5.2 %collective-permute-start.2 = (bf16[2,1,16,16,192]{4,3,2,0,1:T(8,128)(2,1)S(1)}, bf16[2,1,16,16,192]{4,3,2,0,1:T(8,128)(2,1)S(1)}, u32[]{:S(2)}, u32[]{:S(2)}) collective-permute-start(bf16[2,1,16,16,192]{4,3,2,0,1:T(8,128)(2,1)S(1)} %slice.392), channel_id=1, source_target_pairs={{0,8},{8,16},{16,24},{1,9},{9,17},{17,25},{2,10},{10,18},{18,26},{... | collective-permute-start | bytes 589832 | tf_op jit(solution)/shard_map/ppermute | solution.py:13
  48.2 3.8 %copy-start.16 = (f32[192]{0:T(256)S(1)}, f32[192]{0:T(256)}, u32[]{:S(2)}) copy-start(f32[192]{0:T(256)} %param.18) | copy-start | bytes 2308
  48.2 3.8 %copy-start.19 = (f32[192]{0:T(256)S(1)}, f32[192]{0:T(256)}, u32[]{:S(2)}) copy-start(f32[192]{0:T(256)} %param.19) | copy-start | bytes 2308
  62.1 2.0 %copy-start.13 = (bf16[4,16,16,576]{3,2,1,0:T(8,128)(2,1)S(1)}, bf16[4,16,16,576]{3,2,1,0:T(8,128)(2,1)}, u32[]{:S(2)}) copy-start(bf16[4,16,16,576]{3,2,1,0:T(8,128)(2,1)} %get-tuple-element.187) | copy-start | bytes 3538948 | tf_op jit(solution)/shard_map/cond
  64.2 1.3 copy-start.11
  65.5 1.3 copy-start.9
  66.8 1.3 copy-start.7
  68.1 1.3 copy-start.5
  69.4 1.3 copy-start.3
  70.7 1.3 copy-start.1
  107.8 12.4 %collective-permute-start.3 = (bf16[2,1,4,192]{3,2,0,1:T(4,128)(2,1)S(1)}, bf16[2,1,4,192]{3,2,0,1:T(4,128)(2,1)S(1)}, u32[]{:S(2)}, u32[]{:S(2)}) collective-permute-start(bf16[2,1,4,192]{3,2,0,1:T(4,128)(2,1)S(1)} %slice.405), channel_id=1, source_target_pairs={{0,8},{8,16},{16,24},{1,9},{9,17},{17,25},{2,10},{10,18},{18,26},{... | collective-permute-start | bytes 9224 | tf_op jit(solution)/shard_map/ppermute | solution.py:13
  116.3 3.9 %collective-permute-start.4 = (bf16[2,1,4,16,192]{4,3,0,2,1:T(8,128)(2,1)S(1)}, bf16[2,1,4,16,192]{4,3,0,2,1:T(8,128)(2,1)S(1)}, u32[]{:S(2)}, u32[]{:S(2)}) collective-permute-start(bf16[2,1,4,16,192]{4,3,0,2,1:T(8,128)(2,1)S(1)} %slice.408), channel_id=1, source_target_pairs={{0,8},{8,16},{16,24},{1,9},{9,17},{17,25},{2,10},{10,18},{18,26},{... | collective-permute-start | bytes 147464 | tf_op jit(solution)/shard_map/ppermute | solution.py:13
  118.2 5.2 %collective-permute-start.5 = (bf16[2,1,16,16,192]{4,3,2,0,1:T(8,128)(2,1)S(1)}, bf16[2,1,16,16,192]{4,3,2,0,1:T(8,128)(2,1)S(1)}, u32[]{:S(2)}, u32[]{:S(2)}) collective-permute-start(bf16[2,1,16,16,192]{4,3,2,0,1:T(8,128)(2,1)S(1)} %slice_bitcast_fusion.36), channel_id=1, source_target_pairs={{0,8},{8,16},{16,24},{1,9},{9,17},{17,25},{2,10},{10,18},{18,26},{... | collective-permute-start | bytes 589832 | tf_op jit(solution)/shard_map/ppermute | solution.py:13
  120.5 3.9 %copy-start.18 = (f32[192]{0:T(256)S(1)}, f32[192]{0:T(256)}, u32[]{:S(2)}) copy-start(f32[192]{0:T(256)} %param.21) | copy-start | bytes 2308
  134.4 2.0 %copy-start.14 = (bf16[4,16,16,576]{3,2,1,0:T(8,128)(2,1)S(1)}, bf16[4,16,16,576]{3,2,1,0:T(8,128)(2,1)}, u32[]{:S(2)}) copy-start(bf16[4,16,16,576]{3,2,1,0:T(8,128)(2,1)} %get-tuple-element.201) | copy-start | bytes 3538948 | tf_op jit(solution)/shard_map/cond
  136.5 1.3 copy-start.12
  137.8 1.3 copy-start.10
  139.1 1.3 copy-start.8
  140.4 1.3 copy-start.6
  141.7 1.3 copy-start.4
  143.1 1.3 copy-start.2
  144.4 1.3 copy-start
  146.7 1.0 copy-start.15
where the time goes:
time: 150 us; the launch traced here: 149 us
  blocking collectives  58.2 us (39%)
  local copies, waits for them, and re-layouts  33 us (22%)
  starting transfers between devices  25.3 us (17%)
  matrix products  18.2 us (12%)
  other arithmetic  6.69 us (4%)
  waiting for transfers between devices  5.81 us (4%)
    all_gather x2, blocking collectives, extend(): lax.all_gather(edge_pack(activation), 'space', axis=1, tiled=True)  58.2 us
    ppermute x6, starting transfers between devices, shifted(): lax.ppermute(value, axis, [(source, source + steps) for source in range(f...  25.3 us
    dot_general x18, matrix products, conv_tile(): jnp.dot(window, weight[time_off * 3 + row_off], preferred_element_type=jn...  16.4 us
    cond x32, local copies, waits for them, and re-layouts  9.47 us
    slice x2, local copies, waits for them, and re-layouts, conv_tile(): widened[time_off:time_off + frames_out, row_off:row_off + side_len]  8.86 us
    another operation x2, local copies, waits for them, and re-layouts  8.17 us
    ppermute x6, waiting for transfers between devices, shifted(): lax.ppermute(value, axis, [(source, source + steps) for source in range(f...  5.81 us
  transfers between devices with their start and end apart: 6, of which 2 were waited for; matrix products, arithmetic and copies ran while one was open for 1% of the time, Pallas kernels for 0%

commit v1 on v0

--- a/solution.py
+++ b/solution.py
@@ -5,6 +5,19 @@
 from jax.sharding import PartitionSpec as P
 
 epsilon = 1e-06
+
+
+def gather_around(x, axis, dim):
+    ways = lax.axis_size(axis)
+    up = [(d, (d + 1) % ways) for d in range(ways)]
+    down = [(d, (d - 1) % ways) for d in range(ways)]
+    earlier, later = ([x], [x])
+    for _ in range(ways // 2):
+        earlier.append(lax.ppermute(earlier[-1], axis, up))
+    for _ in range((ways - 1) // 2):
+        later.append(lax.ppermute(later[-1], axis, down))
+    line = jnp.concatenate([*earlier[::-1], *later[1:]], axis=dim)
+    return jnp.roll(line, (lax.axis_index(axis) - ways // 2) * x.shape[dim], axis=dim)
 
 
 def shifted(value, axis, steps):
@@ -92,7 +105,7 @@
     folder = partial(fold_edges, nearby=nearby)
     side_rims, corners = folder(
         empty_rims(frames_dev, activation),
-        lax.all_gather(edge_pack(activation), "space", axis=1, tiled=True),
+        gather_around(edge_pack(activation), "space", 1),
         jnp.int32(0),
     )
     prev_act, prev_sides, prev_corners = shifted(

time: 150 us -> 141 us (0.940)
  blocking collectives: 58.2 us -> 0 us
  waiting for transfers between devices: 5.81 us -> 30.3 us
  starting transfers between devices: 25.3 us -> 48.1 us
    all_gather x2 -> x0, blocking collectives: 58.2 us -> none  [extend(): lax.all_gather(edge_pack(activation), 'space', axis=1, tiled=True)]
    ppermute x0 -> x14, starting transfers between devices: none -> 28.6 us  [the longest x6 23.8 us: gather_around(): later.append(lax.ppermute(later[-1], axis, down))]
    ppermute x0 -> x14, waiting for transfers between devices: none -> 27.8 us  [the longest x8 26 us: gather_around(): earlier.append(lax.ppermute(earlier[-1], axis, up))]
    ppermute x6, starting transfers between devices: 25.3 us -> 19.5 us  [shifted(): lax.ppermute(value, axis, [(source, source + steps) for source in range(f...]
    ppermute x6, waiting for transfers between devices: 5.81 us -> 2.53 us  [shifted(): lax.ppermute(value, axis, [(source, source + steps) for source in range(f...]
  transfers between devices with their start and end apart: 6 -> 20, of which waited for: 2 -> 9; matrix products, arithmetic and copies ran while one was open for 1% -> 3% of each run, Pallas kernels for 0% -> 0%
where the time goes in v1:
time: 141 us; the launch traced here: 139 us
  starting transfers between devices  48.1 us (34%)
  local copies, waits for them, and re-layouts  33.2 us (24%)
  waiting for transfers between devices  30.3 us (21%)
  matrix products  18.2 us (13%)
  other arithmetic  7.65 us (5%)
    ppermute x8, waiting for transfers between devices, gather_around(): earlier.append(lax.ppermute(earlier[-1], axis, up))  26 us
    ppermute x6, starting transfers between devices, gather_around(): later.append(lax.ppermute(later[-1], axis, down))  23.8 us
    ppermute x6, starting transfers between devices, shifted(): lax.ppermute(value, axis, [(source, source + steps) for source in range(f...  19.5 us
    dot_general x18, matrix products, conv_tile(): jnp.dot(window, weight[time_off * 3 + row_off], preferred_element_type=jn...  16.4 us
    cond x32, local copies, waits for them, and re-layouts  9.47 us
    slice x2, local copies, waits for them, and re-layouts, conv_tile(): widened[time_off:time_off + frames_out, row_off:row_off + side_len]  8.82 us
    another operation x2, local copies, waits for them, and re-layouts  8.17 us
    ppermute x8, starting transfers between devices, gather_around(): earlier.append(lax.ppermute(earlier[-1], axis, up))  4.78 us
  transfers between devices with their start and end apart: 20, of which 9 were waited for; matrix products, arithmetic and copies ran while one was open for 3% of the time, Pallas kernels for 0%

profile of v1, /device:TPU:1, one launch (start us, length us, event | category | flops | bytes accessed | tf_op | source)
XLA Modules:
  0.0 139.4 jit_solution(15550627138121118230)
XLA Ops:
  0.0 1.6 %reshape.252 = bf16[4,1,16,16,192]{4,3,2,0,1:T(8,128)(2,1)S(1)} reshape(bf16[4,1,16,3072]{3,2,1,0:T(8,128)(2,1)} %param.15) | data formatting | bytes 786432 | tf_op jit(solution)/shard_map/reshape | solution.py:149
  1.6 1.2 dynamic-slice.5
  4.3 2.1 %collective-permute-start = (bf16[4,1,4,16,192]{4,3,2,0,1:T(8,128)(2,1)S(1)}, bf16[4,1,4,16,192]{4,3,2,0,1:T(8,128)(2,1)S(1)}, u32[]{:S(2)}, u32[]{:S(2)}) collective-permute-start(bf16[4,1,4,16,192]{4,3,2,0,1:T(8,128)(2,1)S(1)} %pad_maximum_fusion.4), channel_id=1, source_target_pairs={{0,1},{1,2},{2,3},{3,4},{4,5},{5,6},{6,7},{7,0},{8,9},{9,10},{10,1... | collective-permute-start | bytes 294920 | tf_op jit(solution)/shard_map/ppermute | solution.py:16
  6.5 3.1 %collective-permute-start.4 = (bf16[4,1,4,16,192]{4,3,2,0,1:T(8,128)(2,1)S(1)}, bf16[4,1,4,16,192]{4,3,2,0,1:T(8,128)(2,1)S(1)}, u32[]{:S(2)}, u32[]{:S(2)}) collective-permute-start(bf16[4,1,4,16,192]{4,3,2,0,1:T(8,128)(2,1)S(1)} %pad_maximum_fusion.4), channel_id=1, source_target_pairs={{0,7},{1,0},{2,1},{3,2},{4,3},{5,4},{6,5},{7,6},{8,15},{9,8},{10,9... | collective-permute-start | bytes 294920 | tf_op jit(solution)/shard_map/ppermute | solution.py:18
  9.6 4.1 %collective-permute-start.9 = (bf16[2,1,16,16,192]{4,3,2,0,1:T(8,128)(2,1)S(1)}, bf16[2,1,16,16,192]{4,3,2,0,1:T(8,128)(2,1)S(1)}, u32[]{:S(2)}, u32[]{:S(2)}) collective-permute-start(bf16[2,1,16,16,192]{4,3,2,0,1:T(8,128)(2,1)S(1)} %slice.392), channel_id=1, source_target_pairs={{0,8},{8,16},{16,24},{1,9},{9,17},{17,25},{2,10},{10,18},{18,26},{... | collective-permute-start | bytes 589832 | tf_op jit(solution)/shard_map/ppermute | solution.py:26
  13.7 0.7 fusion.71
  14.6 8.1 %collective-permute-done.1 = bf16[4,1,4,16,192]{4,3,2,0,1:T(8,128)(2,1)S(1)} collective-permute-done((bf16[4,1,4,16,192]{4,3,2,0,1:T(8,128)(2,1)S(1)}, bf16[4,1,4,16,192]{4,3,2,0,1:T(8,128)(2,1)S(1)}, u32[]{:S(2)}, u32[]{:S(2)}) %collective-permute-start.1) | collective-permute-done | bytes 98336 | tf_op jit(solution)/shard_map/ppermute | solution.py:16
  22.7 4.2 %collective-permute-start.5 = (bf16[4,1,4,16,192]{4,3,2,0,1:T(8,128)(2,1)S(1)}, bf16[4,1,4,16,192]{4,3,2,0,1:T(8,128)(2,1)S(1)}, u32[]{:S(2)}, u32[]{:S(2)}) collective-permute-start(bf16[4,1,4,16,192]{4,3,2,0,1:T(8,128)(2,1)S(1)} %collective-permute-done.4), channel_id=1, source_target_pairs={{0,7},{1,0},{2,1},{3,2},{4,3},{5,4},{6,5},{7,6},{8,15},{9,8},{10,9... | collective-permute-start | bytes 294920 | tf_op jit(solution)/shard_map/ppermute | solution.py:18
  26.9 3.1 %collective-permute-done.2 = bf16[4,1,4,16,192]{4,3,2,0,1:T(8,128)(2,1)S(1)} collective-permute-done((bf16[4,1,4,16,192]{4,3,2,0,1:T(8,128)(2,1)S(1)}, bf16[4,1,4,16,192]{4,3,2,0,1:T(8,128)(2,1)S(1)}, u32[]{:S(2)}, u32[]{:S(2)}) %collective-permute-start.2) | collective-permute-done | bytes 98336 | tf_op jit(solution)/shard_map/ppermute | solution.py:16
  30.1 4.1 %collective-permute-start.6 = (bf16[4,1,4,16,192]{4,3,2,0,1:T(8,128)(2,1)S(1)}, bf16[4,1,4,16,192]{4,3,2,0,1:T(8,128)(2,1)S(1)}, u32[]{:S(2)}, u32[]{:S(2)}) collective-permute-start(bf16[4,1,4,16,192]{4,3,2,0,1:T(8,128)(2,1)S(1)} %collective-permute-done.5), channel_id=1, source_target_pairs={{0,7},{1,0},{2,1},{3,2},{4,3},{5,4},{6,5},{7,6},{8,15},{9,8},{10,9... | collective-permute-start | bytes 294920 | tf_op jit(solution)/shard_map/ppermute | solution.py:18
  34.2 2.4 %collective-permute-done.3 = bf16[4,1,4,16,192]{4,3,2,0,1:T(8,128)(2,1)S(1)} collective-permute-done((bf16[4,1,4,16,192]{4,3,2,0,1:T(8,128)(2,1)S(1)}, bf16[4,1,4,16,192]{4,3,2,0,1:T(8,128)(2,1)S(1)}, u32[]{:S(2)}, u32[]{:S(2)}) %collective-permute-start.3) | collective-permute-done | bytes 98336 | tf_op jit(solution)/shard_map/ppermute | solution.py:16
  37.7 3.4 %collective-permute-start.7 = (bf16[2,1,4,192]{3,2,0,1:T(4,128)(2,1)S(1)}, bf16[2,1,4,192]{3,2,0,1:T(4,128)(2,1)S(1)}, u32[]{:S(2)}, u32[]{:S(2)}) collective-permute-start(bf16[2,1,4,192]{3,2,0,1:T(4,128)(2,1)S(1)} %slice.382), channel_id=1, source_target_pairs={{0,8},{8,16},{16,24},{1,9},{9,17},{17,25},{2,10},{10,18},{18,26},{... | collective-permute-start | bytes 9224 | tf_op jit(solution)/shard_map/ppermute | solution.py:26
  41.1 0.7 fusion.14
  41.9 1.9 %collective-permute-start.8 = (bf16[2,1,4,16,192]{4,3,0,2,1:T(8,128)(2,1)S(1)}, bf16[2,1,4,16,192]{4,3,0,2,1:T(8,128)(2,1)S(1)}, u32[]{:S(2)}, u32[]{:S(2)}) collective-permute-start(bf16[2,1,4,16,192]{4,3,0,2,1:T(8,128)(2,1)S(1)} %slice.385), channel_id=1, source_target_pairs={{0,8},{8,16},{16,24},{1,9},{9,17},{17,25},{2,10},{10,18},{18,26},{... | collective-permute-start | bytes 147464 | tf_op jit(solution)/shard_map/ppermute | solution.py:26
  43.9 1.3 collective-permute-done.8
  45.5 0.9 pad_maximum_fusion.2
  46.4 24.9 %conditional.2 = (bf16[4,16,16,192]{3,2,1,0:T(8,128)(2,1)S(1)}) conditional(s32[]{:T(128)} %convert_element_type.107, () %tuple.21, (bf16[6,1,18,18,192]{4,3,2,0,1:T(8,128)(2,1)S(1)}, bf16[9,576,192]{1,2,0:T(8,128)(2,1)}, f32[192]{0:T(256)S(1)}, s32[]{:T(128)}, s32[4]{0:T(128)S(1)}, /*index=5*/f32[192]{0:T(256)S(1)}) %tuple.101), branch_computations={%region_1.3_spmd, %region_2.5_spmd} | conditional | flops 2048533504 | bytes 96561936 | solution.py:132
  46.6 0.7 fusion.75
  47.3 0.9 pad_maximum_fusion
  48.1 4.4 %fusion.74 = (bf16[4,16,16,576]{3,2,1,0:T(8,128)(2,1)}, bf16[4,16,16,576]{3,2,1,0:T(8,128)(2,1)}, bf16[4,16,16,576]{3,2,1,0:T(8,128)(2,1)}, bf16[4,16,16,576]{3,...) fusion(bf16[6,18,16,576]{3,2,1,0:T(8,128)(2,1)S(1)} %pad_maximu, ...), kind=kLoop, calls=%fused_computation.197 | loop fusion | bytes 21233664 | tf_op jit(solution)/shard_map/cond/branch_1_fun/slice | solution.py:44
  52.5 4.1 %copy.153 = bf16[9,576,192]{2,1,0:T(8,128)(2,1)S(1)} copy(bf16[9,576,192]{1,2,0:T(8,128)(2,1)} %get-tuple-element.156) | data formatting | bytes 3981312 | tf_op jit(solution)/shard_map
  56.6 2.0 %fusion = f32[1024,192]{0,1:T(8,128)S(1)} fusion(bf16[1024,576]{1,0:T(8,128)(2,1)} %bitcast.249, bf16[9,576,192]{2,1,0:T(8,128)(2,1)S(1)} %copy.153), kind=kOutput, calls=%fused_computation.20 | convolution fusion | flops 226492416 | bytes 2260992 | tf_op jit(solution)/shard_map/cond/branch_1_fun/dot_general | solution.py:47
  58.7 0.6 convolution_add_fusion.7
  59.3 0.7 copy-done.11
  60.0 0.6 convolution_add_fusion.6
  60.6 0.7 copy-done.9
  61.9 0.7 copy-done.7
  63.2 0.7 copy-done.5
  64.6 0.7 copy-done.3
  65.9 0.7 copy-done.1
  66.6 1.5 %convolution_add_fusion.1 = f32[1024,192]{0,1:T(8,128)} fusion(f32[1024,192]{0,1:T(8,128)S(1)} %convolution_add_fusion.2, bf16[1024,576]{1,0:T(8,128)(2,1)S(1)} %bitcast.235, bf16[9,576,192]{2,1,0:T(8,128)(2,1)S(1)} %copy.153), kind=kOutput, calls=%fused_computation.2 | convolution fusion | flops 226689024 | bytes 3178496 | tf_op jit(solution)/shard_map/cond/branch_1_fun/dot_general | solution.py:47
  68.2 2.2 %multiply_reduce_fusion = (f32[1024]{0:T(1024)S(1)}, f32[1024,192]{0,1:T(8,128)S(1)}) fusion(f32[1024]{0:T(1024)S(1)} %mul.124, f32[192]{0:T(256)S(1)} %get-tuple-element.61, f32[1024,192]{0,1:T(8,128)} %convolution_add_fusion.1, bf16[1024,576]{1,0:T(8,128)(2,1)} %bitcast.233, bf16[9,576,192]{2,1,0:T(8,128)(2,1)S(1)} %copy.153), kind=kOutput, calls=%fused_computation.10 | convolution fusion | flops 227474432 | bytes 3056640 | tf_op jit(solution)/shard_map/cond/branch_1_fun/dot_general | solution.py:47
  71.4 1.0 collective-permute-start.10
  72.5 7.0 %collective-permute-done.10 = bf16[4,1,4,16,192]{4,3,2,0,1:T(8,128)(2,1)S(1)} collective-permute-done((bf16[4,1,4,16,192]{4,3,2,0,1:T(8,128)(2,1)S(1)}, bf16[4,1,4,16,192]{4,3,2,0,1:T(8,128)(2,1)S(1)}, u32[]{:S(2)}, u32[]{:S(2)}) %collective-permute-start.10) | collective-permute-done | bytes 98336 | tf_op jit(solution)/shard_map/ppermute | solution.py:16
  79.5 4.2 %collective-permute-start.14 = (bf16[4,1,4,16,192]{4,3,2,0,1:T(8,128)(2,1)S(1)}, bf16[4,1,4,16,192]{4,3,2,0,1:T(8,128)(2,1)S(1)}, u32[]{:S(2)}, u32[]{:S(2)}) collective-permute-start(bf16[4,1,4,16,192]{4,3,2,0,1:T(8,128)(2,1)S(1)} %pad_maximum_fusion.5), channel_id=1, source_target_pairs={{0,7},{1,0},{2,1},{3,2},{4,3},{5,4},{6,5},{7,6},{8,15},{9,8},{10,9... | collective-permute-start | bytes 294920 | tf_op jit(solution)/shard_map/ppermute | solution.py:18
  83.7 2.8 %collective-permute-done.11 = bf16[4,1,4,16,192]{4,3,2,0,1:T(8,128)(2,1)S(1)} collective-permute-done((bf16[4,1,4,16,192]{4,3,2,0,1:T(8,128)(2,1)S(1)}, bf16[4,1,4,16,192]{4,3,2,0,1:T(8,128)(2,1)S(1)}, u32[]{:S(2)}, u32[]{:S(2)}) %collective-permute-start.11) | collective-permute-done | bytes 98336 | tf_op jit(solution)/shard_map/ppermute | solution.py:16
  86.9 3.8 %collective-permute-start.15 = (bf16[4,1,4,16,192]{4,3,2,0,1:T(8,128)(2,1)S(1)}, bf16[4,1,4,16,192]{4,3,2,0,1:T(8,128)(2,1)S(1)}, u32[]{:S(2)}, u32[]{:S(2)}) collective-permute-start(bf16[4,1,4,16,192]{4,3,2,0,1:T(8,128)(2,1)S(1)} %collective-permute-done.14), channel_id=1, source_target_pairs={{0,7},{1,0},{2,1},{3,2},{4,3},{5,4},{6,5},{7,6},{8,15},{9,8},{10,9... | collective-permute-start | bytes 294920 | tf_op jit(solution)/shard_map/ppermute | solution.py:18
  90.6 2.4 %collective-permute-done.12 = bf16[4,1,4,16,192]{4,3,2,0,1:T(8,128)(2,1)S(1)} collective-permute-done((bf16[4,1,4,16,192]{4,3,2,0,1:T(8,128)(2,1)S(1)}, bf16[4,1,4,16,192]{4,3,2,0,1:T(8,128)(2,1)S(1)}, u32[]{:S(2)}, u32[]{:S(2)}) %collective-permute-start.12) | collective-permute-done | bytes 98336 | tf_op jit(solution)/shard_map/ppermute | solution.py:16
  93.1 1.1 collective-permute-start.13
  94.2 5.4 %collective-permute-start.19 = (bf16[2,1,16,16,192]{4,3,2,0,1:T(8,128)(2,1)S(1)}, bf16[2,1,16,16,192]{4,3,2,0,1:T(8,128)(2,1)S(1)}, u32[]{:S(2)}, u32[]{:S(2)}) collective-permute-start(bf16[2,1,16,16,192]{4,3,2,0,1:T(8,128)(2,1)S(1)} %slice_bitcast_fusion.36), channel_id=1, source_target_pairs={{0,8},{8,16},{16,24},{1,9},{9,17},{17,25},{2,10},{10,18},{18,26},{... | collective-permute-start | bytes 589832 | tf_op jit(solution)/shard_map/ppermute | solution.py:26
  99.6 4.5 %collective-permute-start.16 = (bf16[4,1,4,16,192]{4,3,2,0,1:T(8,128)(2,1)S(1)}, bf16[4,1,4,16,192]{4,3,2,0,1:T(8,128)(2,1)S(1)}, u32[]{:S(2)}, u32[]{:S(2)}) collective-permute-start(bf16[4,1,4,16,192]{4,3,2,0,1:T(8,128)(2,1)S(1)} %collective-permute-done.15), channel_id=1, source_target_pairs={{0,7},{1,0},{2,1},{3,2},{4,3},{5,4},{6,5},{7,6},{8,15},{9,8},{10,9... | collective-permute-start | bytes 294920 | tf_op jit(solution)/shard_map/ppermute | solution.py:18
  104.2 1.8 %collective-permute-done.16 = bf16[4,1,4,16,192]{4,3,2,0,1:T(8,128)(2,1)S(1)} collective-permute-done((bf16[4,1,4,16,192]{4,3,2,0,1:T(8,128)(2,1)S(1)}, bf16[4,1,4,16,192]{4,3,2,0,1:T(8,128)(2,1)S(1)}, u32[]{:S(2)}, u32[]{:S(2)}) %collective-permute-start.16) | collective-permute-done | bytes 98336 | tf_op jit(solution)/shard_map/ppermute | solution.py:18
  106.9 2.8 %collective-permute-start.17 = (bf16[2,1,4,192]{3,2,0,1:T(4,128)(2,1)S(1)}, bf16[2,1,4,192]{3,2,0,1:T(4,128)(2,1)S(1)}, u32[]{:S(2)}, u32[]{:S(2)}) collective-permute-start(bf16[2,1,4,192]{3,2,0,1:T(4,128)(2,1)S(1)} %slice.405), channel_id=1, source_target_pairs={{0,8},{8,16},{16,24},{1,9},{9,17},{17,25},{2,10},{10,18},{18,26},{... | collective-permute-start | bytes 9224 | tf_op jit(solution)/shard_map/ppermute | solution.py:26
  109.7 0.7 fusion.12
  110.5 1.9 %collective-permute-start.18 = (bf16[2,1,4,16,192]{4,3,0,2,1:T(8,128)(2,1)S(1)}, bf16[2,1,4,16,192]{4,3,0,2,1:T(8,128)(2,1)S(1)}, u32[]{:S(2)}, u32[]{:S(2)}) collective-permute-start(bf16[2,1,4,16,192]{4,3,0,2,1:T(8,128)(2,1)S(1)} %slice.408), channel_id=1, source_target_pairs={{0,8},{8,16},{16,24},{1,9},{9,17},{17,25},{2,10},{10,18},{18,26},{... | collective-permute-start | bytes 147464 | tf_op jit(solution)/shard_map/ppermute | solution.py:26
  112.4 1.3 collective-permute-done.18
  114.0 0.9 pad_maximum_fusion.3
  114.9 24.5 %conditional.3 = (bf16[4,1,16,3072]{3,2,0,1:T(8,128)(2,1)}) conditional(s32[]{:T(128)} %convert_element_type.107, () %tuple.20, (bf16[6,1,18,18,192]{4,3,2,0,1:T(8,128)(2,1)S(1)}, bf16[9,576,192]{1,2,0:T(8,128)(2,1)}, f32[192]{0:T(256)S(1)}, s32[]{:T(128)}, s32[4]{0:T(128)S(1)}, /*index=5*/bf16[4]{0:T(256)(128)(2,1)S(1)}, ...), branch_computations={%region_4.6_spmd, %region_5.7_spmd} | conditional | flops 2047156224 | bytes 104957008 | solution.py:132
  115.1 0.7 fusion.77
  115.8 0.9 pad_maximum_fusion.1
  116.7 4.4 %fusion.76 = (bf16[4,16,16,576]{3,2,1,0:T(8,128)(2,1)}, bf16[4,16,16,576]{3,2,1,0:T(8,128)(2,1)}, bf16[4,16,16,576]{3,2,1,0:T(8,128)(2,1)}, bf16[4,16,16,576]{3,...) fusion(bf16[6,18,16,576]{3,2,1,0:T(8,128)(2,1)S(1)} %pad_maximu, ...), kind=kLoop, calls=%fused_computation.199 | loop fusion | bytes 21233664 | tf_op jit(solution)/shard_map/cond/branch_1_fun/slice | solution.py:44
  121.1 4.1 %copy.164 = bf16[9,576,192]{2,1,0:T(8,128)(2,1)S(1)} copy(bf16[9,576,192]{1,2,0:T(8,128)(2,1)} %get-tuple-element.162) | data formatting | bytes 3981312 | tf_op jit(solution)/shard_map
  125.2 2.0 %fusion.1 = f32[1024,192]{0,1:T(8,128)S(1)} fusion(bf16[1024,576]{1,0:T(8,128)(2,1)} %bitcast.250, bf16[9,576,192]{2,1,0:T(8,128)(2,1)S(1)} %copy.164), kind=kOutput, calls=%fused_computation.43 | convolution fusion | flops 226492416 | bytes 2260992 | tf_op jit(solution)/shard_map/cond/branch_1_fun/dot_general | solution.py:47
  127.2 0.6 convolution_add_fusion.15
  127.9 0.7 copy-done.12
  128.6 0.6 convolution_add_fusion.14
  129.2 0.7 copy-done.10
  130.5 0.7 copy-done.8
  131.8 0.7 copy-done.6
  133.1 0.7 copy-done.4
  134.4 0.7 copy-done.2
  135.8 0.7 copy-done
  136.5 0.6 convolution_add_fusion.8
  138.4 0.9 add_convert_fusion
  (135 shorter events, 12.0 us)
Async XLA Ops:
  0.0 3.7 %copy-start.17 = (f32[192]{0:T(256)S(1)}, f32[192]{0:T(256)}, u32[]{:S(2)}) copy-start(f32[192]{0:T(256)} %param.18) | copy-start | bytes 2308
  4.3 10.1 %collective-permute-start = (bf16[4,1,4,16,192]{4,3,2,0,1:T(8,128)(2,1)S(1)}, bf16[4,1,4,16,192]{4,3,2,0,1:T(8,128)(2,1)S(1)}, u32[]{:S(2)}, u32[]{:S(2)}) collective-permute-start(bf16[4,1,4,16,192]{4,3,2,0,1:T(8,128)(2,1)S(1)} %pad_maximum_fusion.4), channel_id=1, source_target_pairs={{0,1},{1,2},{2,3},{3,4},{4,5},{5,6},{6,7},{7,0},{8,9},{9,10},{10,1... | collective-permute-start | bytes 294920 | tf_op jit(solution)/shard_map/ppermute | solution.py:16
  6.5 16.3 %collective-permute-start.4 = (bf16[4,1,4,16,192]{4,3,2,0,1:T(8,128)(2,1)S(1)}, bf16[4,1,4,16,192]{4,3,2,0,1:T(8,128)(2,1)S(1)}, u32[]{:S(2)}, u32[]{:S(2)}) collective-permute-start(bf16[4,1,4,16,192]{4,3,2,0,1:T(8,128)(2,1)S(1)} %pad_maximum_fusion.4), channel_id=1, source_target_pairs={{0,7},{1,0},{2,1},{3,2},{4,3},{5,4},{6,5},{7,6},{8,15},{9,8},{10,9... | collective-permute-start | bytes 294920 | tf_op jit(solution)/shard_map/ppermute | solution.py:18
  9.6 35.9 %collective-permute-start.9 = (bf16[2,1,16,16,192]{4,3,2,0,1:T(8,128)(2,1)S(1)}, bf16[2,1,16,16,192]{4,3,2,0,1:T(8,128)(2,1)S(1)}, u32[]{:S(2)}, u32[]{:S(2)}) collective-permute-start(bf16[2,1,16,16,192]{4,3,2,0,1:T(8,128)(2,1)S(1)} %slice.392), channel_id=1, source_target_pairs={{0,8},{8,16},{16,24},{1,9},{9,17},{17,25},{2,10},{10,18},{18,26},{... | collective-permute-start | bytes 589832 | tf_op jit(solution)/shard_map/ppermute | solution.py:26
  14.5 8.2 %collective-permute-start.1 = (bf16[4,1,4,16,192]{4,3,2,0,1:T(8,128)(2,1)S(1)}, bf16[4,1,4,16,192]{4,3,2,0,1:T(8,128)(2,1)S(1)}, u32[]{:S(2)}, u32[]{:S(2)}) collective-permute-start(bf16[4,1,4,16,192]{4,3,2,0,1:T(8,128)(2,1)S(1)} %collective-permute-done), channel_id=1, source_target_pairs={{0,1},{1,2},{2,3},{3,4},{4,5},{5,6},{6,7},{7,0},{8,9},{9,10},{10,1... | collective-permute-start | bytes 294920 | tf_op jit(solution)/shard_map/ppermute | solution.py:16
  22.7 7.4 %collective-permute-start.2 = (bf16[4,1,4,16,192]{4,3,2,0,1:T(8,128)(2,1)S(1)}, bf16[4,1,4,16,192]{4,3,2,0,1:T(8,128)(2,1)S(1)}, u32[]{:S(2)}, u32[]{:S(2)}) collective-permute-start(bf16[4,1,4,16,192]{4,3,2,0,1:T(8,128)(2,1)S(1)} %collective-permute-done.1), channel_id=1, source_target_pairs={{0,1},{1,2},{2,3},{3,4},{4,5},{5,6},{6,7},{7,0},{8,9},{9,10},{10,1... | collective-permute-start | bytes 294920 | tf_op jit(solution)/shard_map/ppermute | solution.py:16
  22.7 7.4 %collective-permute-start.5 = (bf16[4,1,4,16,192]{4,3,2,0,1:T(8,128)(2,1)S(1)}, bf16[4,1,4,16,192]{4,3,2,0,1:T(8,128)(2,1)S(1)}, u32[]{:S(2)}, u32[]{:S(2)}) collective-permute-start(bf16[4,1,4,16,192]{4,3,2,0,1:T(8,128)(2,1)S(1)} %collective-permute-done.4), channel_id=1, source_target_pairs={{0,7},{1,0},{2,1},{3,2},{4,3},{5,4},{6,5},{7,6},{8,15},{9,8},{10,9... | collective-permute-start | bytes 294920 | tf_op jit(solution)/shard_map/ppermute | solution.py:18
  30.1 6.6 %collective-permute-start.3 = (bf16[4,1,4,16,192]{4,3,2,0,1:T(8,128)(2,1)S(1)}, bf16[4,1,4,16,192]{4,3,2,0,1:T(8,128)(2,1)S(1)}, u32[]{:S(2)}, u32[]{:S(2)}) collective-permute-start(bf16[4,1,4,16,192]{4,3,2,0,1:T(8,128)(2,1)S(1)} %collective-permute-done.2), channel_id=1, source_target_pairs={{0,1},{1,2},{2,3},{3,4},{4,5},{5,6},{6,7},{7,0},{8,9},{9,10},{10,1... | collective-permute-start | bytes 294920 | tf_op jit(solution)/shard_map/ppermute | solution.py:16
  30.1 6.7 %collective-permute-start.6 = (bf16[4,1,4,16,192]{4,3,2,0,1:T(8,128)(2,1)S(1)}, bf16[4,1,4,16,192]{4,3,2,0,1:T(8,128)(2,1)S(1)}, u32[]{:S(2)}, u32[]{:S(2)}) collective-permute-start(bf16[4,1,4,16,192]{4,3,2,0,1:T(8,128)(2,1)S(1)} %collective-permute-done.5), channel_id=1, source_target_pairs={{0,7},{1,0},{2,1},{3,2},{4,3},{5,4},{6,5},{7,6},{8,15},{9,8},{10,9... | collective-permute-start | bytes 294920 | tf_op jit(solution)/shard_map/ppermute | solution.py:18
  37.7 6.2 %collective-permute-start.7 = (bf16[2,1,4,192]{3,2,0,1:T(4,128)(2,1)S(1)}, bf16[2,1,4,192]{3,2,0,1:T(4,128)(2,1)S(1)}, u32[]{:S(2)}, u32[]{:S(2)}) collective-permute-start(bf16[2,1,4,192]{3,2,0,1:T(4,128)(2,1)S(1)} %slice.382), channel_id=1, source_target_pairs={{0,8},{8,16},{16,24},{1,9},{9,17},{17,25},{2,10},{10,18},{18,26},{... | collective-permute-start | bytes 9224 | tf_op jit(solution)/shard_map/ppermute | solution.py:26
  41.9 3.2 %collective-permute-start.8 = (bf16[2,1,4,16,192]{4,3,0,2,1:T(8,128)(2,1)S(1)}, bf16[2,1,4,16,192]{4,3,0,2,1:T(8,128)(2,1)S(1)}, u32[]{:S(2)}, u32[]{:S(2)}) collective-permute-start(bf16[2,1,4,16,192]{4,3,0,2,1:T(8,128)(2,1)S(1)} %slice.385), channel_id=1, source_target_pairs={{0,8},{8,16},{16,24},{1,9},{9,17},{17,25},{2,10},{10,18},{18,26},{... | collective-permute-start | bytes 147464 | tf_op jit(solution)/shard_map/ppermute | solution.py:26
  45.4 1.0 copy-start.16
  45.4 1.0 copy-start.19
  56.6 2.0 %copy-start.13 = (bf16[4,16,16,576]{3,2,1,0:T(8,128)(2,1)S(1)}, bf16[4,16,16,576]{3,2,1,0:T(8,128)(2,1)}, u32[]{:S(2)}) copy-start(bf16[4,16,16,576]{3,2,1,0:T(8,128)(2,1)} %get-tuple-element.175) | copy-start | bytes 3538948 | tf_op jit(solution)/shard_map/cond
  58.7 1.3 copy-start.11
  60.0 1.3 copy-start.9
  61.3 1.3 copy-start.7
  62.6 1.3 copy-start.5
  63.9 1.3 copy-start.3
  65.2 1.3 copy-start.1
  71.4 8.1 %collective-permute-start.10 = (bf16[4,1,4,16,192]{4,3,2,0,1:T(8,128)(2,1)S(1)}, bf16[4,1,4,16,192]{4,3,2,0,1:T(8,128)(2,1)S(1)}, u32[]{:S(2)}, u32[]{:S(2)}) collective-permute-start(bf16[4,1,4,16,192]{4,3,2,0,1:T(8,128)(2,1)S(1)} %pad_maximum_fusion.5), channel_id=1, source_target_pairs={{0,1},{1,2},{2,3},{3,4},{4,5},{5,6},{6,7},{7,0},{8,9},{9,10},{10,1... | collective-permute-start | bytes 294920 | tf_op jit(solution)/shard_map/ppermute | solution.py:16
  79.5 7.0 %collective-permute-start.11 = (bf16[4,1,4,16,192]{4,3,2,0,1:T(8,128)(2,1)S(1)}, bf16[4,1,4,16,192]{4,3,2,0,1:T(8,128)(2,1)S(1)}, u32[]{:S(2)}, u32[]{:S(2)}) collective-permute-start(bf16[4,1,4,16,192]{4,3,2,0,1:T(8,128)(2,1)S(1)} %collective-permute-done.10), channel_id=1, source_target_pairs={{0,1},{1,2},{2,3},{3,4},{4,5},{5,6},{6,7},{7,0},{8,9},{9,10},{10,1... | collective-permute-start | bytes 294920 | tf_op jit(solution)/shard_map/ppermute | solution.py:16
  79.5 7.4 %collective-permute-start.14 = (bf16[4,1,4,16,192]{4,3,2,0,1:T(8,128)(2,1)S(1)}, bf16[4,1,4,16,192]{4,3,2,0,1:T(8,128)(2,1)S(1)}, u32[]{:S(2)}, u32[]{:S(2)}) collective-permute-start(bf16[4,1,4,16,192]{4,3,2,0,1:T(8,128)(2,1)S(1)} %pad_maximum_fusion.5), channel_id=1, source_target_pairs={{0,7},{1,0},{2,1},{3,2},{4,3},{5,4},{6,5},{7,6},{8,15},{9,8},{10,9... | collective-permute-start | bytes 294920 | tf_op jit(solution)/shard_map/ppermute | solution.py:18
  86.5 6.6 %collective-permute-start.12 = (bf16[4,1,4,16,192]{4,3,2,0,1:T(8,128)(2,1)S(1)}, bf16[4,1,4,16,192]{4,3,2,0,1:T(8,128)(2,1)S(1)}, u32[]{:S(2)}, u32[]{:S(2)}) collective-permute-start(bf16[4,1,4,16,192]{4,3,2,0,1:T(8,128)(2,1)S(1)} %collective-permute-done.11), channel_id=1, source_target_pairs={{0,1},{1,2},{2,3},{3,4},{4,5},{5,6},{6,7},{7,0},{8,9},{9,10},{10,1... | collective-permute-start | bytes 294920 | tf_op jit(solution)/shard_map/ppermute | solution.py:16
  86.9 12.7 %collective-permute-start.15 = (bf16[4,1,4,16,192]{4,3,2,0,1:T(8,128)(2,1)S(1)}, bf16[4,1,4,16,192]{4,3,2,0,1:T(8,128)(2,1)S(1)}, u32[]{:S(2)}, u32[]{:S(2)}) collective-permute-start(bf16[4,1,4,16,192]{4,3,2,0,1:T(8,128)(2,1)S(1)} %collective-permute-done.14), channel_id=1, source_target_pairs={{0,7},{1,0},{2,1},{3,2},{4,3},{5,4},{6,5},{7,6},{8,15},{9,8},{10,9... | collective-permute-start | bytes 294920 | tf_op jit(solution)/shard_map/ppermute | solution.py:18
  93.1 11.0 %collective-permute-start.13 = (bf16[4,1,4,16,192]{4,3,2,0,1:T(8,128)(2,1)S(1)}, bf16[4,1,4,16,192]{4,3,2,0,1:T(8,128)(2,1)S(1)}, u32[]{:S(2)}, u32[]{:S(2)}) collective-permute-start(bf16[4,1,4,16,192]{4,3,2,0,1:T(8,128)(2,1)S(1)} %collective-permute-done.12), channel_id=1, source_target_pairs={{0,1},{1,2},{2,3},{3,4},{4,5},{5,6},{6,7},{7,0},{8,9},{9,10},{10,1... | collective-permute-start | bytes 294920 | tf_op jit(solution)/shard_map/ppermute | solution.py:16
  94.2 19.8 %collective-permute-start.19 = (bf16[2,1,16,16,192]{4,3,2,0,1:T(8,128)(2,1)S(1)}, bf16[2,1,16,16,192]{4,3,2,0,1:T(8,128)(2,1)S(1)}, u32[]{:S(2)}, u32[]{:S(2)}) collective-permute-start(bf16[2,1,16,16,192]{4,3,2,0,1:T(8,128)(2,1)S(1)} %slice_bitcast_fusion.36), channel_id=1, source_target_pairs={{0,8},{8,16},{16,24},{1,9},{9,17},{17,25},{2,10},{10,18},{18,26},{... | collective-permute-start | bytes 589832 | tf_op jit(solution)/shard_map/ppermute | solution.py:26
  99.6 6.4 %collective-permute-start.16 = (bf16[4,1,4,16,192]{4,3,2,0,1:T(8,128)(2,1)S(1)}, bf16[4,1,4,16,192]{4,3,2,0,1:T(8,128)(2,1)S(1)}, u32[]{:S(2)}, u32[]{:S(2)}) collective-permute-start(bf16[4,1,4,16,192]{4,3,2,0,1:T(8,128)(2,1)S(1)} %collective-permute-done.15), channel_id=1, source_target_pairs={{0,7},{1,0},{2,1},{3,2},{4,3},{5,4},{6,5},{7,6},{8,15},{9,8},{10,9... | collective-permute-start | bytes 294920 | tf_op jit(solution)/shard_map/ppermute | solution.py:18
  106.9 5.5 %collective-permute-start.17 = (bf16[2,1,4,192]{3,2,0,1:T(4,128)(2,1)S(1)}, bf16[2,1,4,192]{3,2,0,1:T(4,128)(2,1)S(1)}, u32[]{:S(2)}, u32[]{:S(2)}) collective-permute-start(bf16[2,1,4,192]{3,2,0,1:T(4,128)(2,1)S(1)} %slice.405), channel_id=1, source_target_pairs={{0,8},{8,16},{16,24},{1,9},{9,17},{17,25},{2,10},{10,18},{18,26},{... | collective-permute-start | bytes 9224 | tf_op jit(solution)/shard_map/ppermute | solution.py:26
  110.5 3.2 %collective-permute-start.18 = (bf16[2,1,4,16,192]{4,3,0,2,1:T(8,128)(2,1)S(1)}, bf16[2,1,4,16,192]{4,3,0,2,1:T(8,128)(2,1)S(1)}, u32[]{:S(2)}, u32[]{:S(2)}) collective-permute-start(bf16[2,1,4,16,192]{4,3,0,2,1:T(8,128)(2,1)S(1)} %slice.408), channel_id=1, source_target_pairs={{0,8},{8,16},{16,24},{1,9},{9,17},{17,25},{2,10},{10,18},{18,26},{... | collective-permute-start | bytes 147464 | tf_op jit(solution)/shard_map/ppermute | solution.py:26
  113.9 0.9 copy-start.18
  125.2 2.0 %copy-start.14 = (bf16[4,16,16,576]{3,2,1,0:T(8,128)(2,1)S(1)}, bf16[4,16,16,576]{3,2,1,0:T(8,128)(2,1)}, u32[]{:S(2)}) copy-start(bf16[4,16,16,576]{3,2,1,0:T(8,128)(2,1)} %get-tuple-element.189) | copy-start | bytes 3538948 | tf_op jit(solution)/shard_map/cond
  127.2 1.3 copy-start.12
  128.6 1.3 copy-start.10
  129.9 1.3 copy-start.8
  131.2 1.3 copy-start.6
  132.5 1.3 copy-start.4
  133.8 1.3 copy-start.2
  135.1 1.3 copy-start
  137.4 1.0 copy-start.15
